TPU v7x, 32 devices: a whole 2x2x4 slice. The times are simulated.
32 devices in a mesh: seq: 16 (over z, y, x), tp: 2 (over core).
Axes of the slice: x: 2, y: 2, z: 4, core: 2. Of those that a mesh axis runs over, the one named last changes fastest.
Arguments:
- tokens: bfloat16 [2048, 2048], P('seq'), may hold values from -6 to 6
- attn_gain: float32 [2048], replicated, may hold values from 0.1 to 1.9
- mlp_gain: float32 [2048], replicated, may hold values from 0.1 to 1.9
- w_query: float32 [2048, 2048], P('seq', 'tp'), may hold values from -0.70710678 to 0.70710678
- w_key: float32 [2048, 2048], P('seq', 'tp'), may hold values from -0.70710678 to 0.70710678
- w_value: float32 [2048, 2048], P('seq', 'tp'), may hold values from -0.125 to 0.125
- w_out: float32 [2048, 2048], P('tp', 'seq'), may hold values from -0.125 to 0.125
- sink_logits: float32 [16], P('tp'), may hold values from 8 to 16
- router: float32 [2048, 16], P('seq'), may hold values from -0.25 to 0.25
- expert_gate: float32 [16, 2048, 1024], P(None, 'seq', 'tp'), may hold values from -0.125 to 0.125
- expert_up: float32 [16, 2048, 1024], P(None, 'seq', 'tp'), may hold values from -0.125 to 0.125
- expert_down: float32 [16, 2048, 1024], P(None, 'seq', 'tp'), may hold values from -0.1875 to 0.1875
- layout_map: int32 [16], replicated, may hold values from 0 to 15, each once
- real_lengths: int32 [2], replicated, may hold values from 256 to 1088, as said below
- routes: int32 [2048, 8], P('seq'), may hold values from 0 to 15, all different within a row; in each aligned block of 128 rows (0 to 127, 128 to 255, ...) at most 72 rows name the same one
Outputs:
- layer_out: bfloat16 [2048, 2048], P('seq', 'tp')
Inputs may be any that keep to these rules, and one draw needn't show every extreme that they name: Prompt p has real tokens in the first real_lengths[p] of its slots and padding after them; each length is at least 256; the last prompt has no padding. `routes`: each row names 8 different experts; among the rows of one device no expert is named more than 72 times, and in some device some expert exactly 72 times. `layout_map`: each trainer expert is held by exactly one server expert number.
All inputs are finite; a program needn't handle non-finite values.
Results may differ from a plain program's by a relative error of at most 0.0075.
The roundings to bfloat16 on the way count: a program that leaves them out, or rounds other values in their place, can miss the bound.
Values may be sent and summed in bfloat16 or wider, within the bound.
No kernel may reach another device: no remote copies, remote signals or barrier semaphores. Data moves between devices by JAX's collectives and lax.ppermute only.
A program may use at most 128 MiB of HBM per device.

v0:
```python
import jax
import jax.numpy as jnp
from jax import lax
from jax.sharding import PartitionSpec as P

HEAD = 128
HALF_WIN = 2048
EPSILON = 1e-05
ROPE_BASE = 50000.0
MASKED = -1e30


def from_behind(value, axis, steps):
    count = lax.axis_size(axis)
    first, last = (max(0, -steps), min(count, count - steps))
    return lax.ppermute(value, axis, [(source, source + steps) for source in range(first, last)])


def rms_scale(row_values, gain_vector):
    mean_square = jnp.mean(row_values * row_values, axis=-1, keepdims=True)
    return row_values * lax.rsqrt(mean_square + EPSILON) * gain_vector


def rotate(head_block, positions):
    half_dim = head_block.shape[-1] // 2
    frequency = ROPE_BASE ** (-jnp.arange(half_dim, dtype=jnp.float32) / half_dim)
    angles = positions[:, None, None] * frequency[None, None, :]
    cosine = jnp.cos(angles)
    sine_part = jnp.sin(angles)
    first_half = head_block[..., :half_dim]
    second_half = head_block[..., half_dim:]
    return jnp.concatenate(
        [
            first_half * cosine - second_half * sine_part,
            second_half * cosine + first_half * sine_part,
        ],
        axis=-1,
    )


def length_of(prompt, real_lengths):
    one_hot = prompt[:, None] == jnp.arange(real_lengths.shape[0], dtype=jnp.int32)[None, :]
    return jnp.sum(jnp.where(one_hot, real_lengths[None, :], 0), axis=1)


def prompt_split(slot_ids, slot_len, stagger, prompt_count):
    prompt = jnp.minimum((slot_ids + stagger) // slot_len, prompt_count - 1)
    start = jnp.maximum(prompt * slot_len - stagger, 0)
    return (prompt, slot_ids - start)


def key_rules(query_ids, key_ids, slot_len, stagger, total_slots, real_lengths):
    prompt_count = real_lengths.shape[0]
    key_prompt, key_pos = prompt_split(key_ids, slot_len, stagger, prompt_count)
    query_prompt = prompt_split(query_ids, slot_len, stagger, prompt_count)[0]
    inside = (key_ids >= 0) & (key_ids < total_slots)
    key_live = inside & (key_pos < length_of(key_prompt, real_lengths))
    same_prompt = query_prompt[:, None] == key_prompt[None, :]
    nearby = jnp.abs(query_ids[:, None] - key_ids[None, :]) < HALF_WIN
    return same_prompt & nearby & key_live[None, :]


def attend(softmax_state, query_rows, key_rows, value_rows, allowed):
    running_max, denominator, accumulated = softmax_state
    scores = jnp.einsum(
        "tge,kge->gtk", query_rows, key_rows, preferred_element_type=jnp.float32
    ) * HEAD ** (-0.5)
    scores = jnp.where(allowed[None], scores, MASKED)
    new_max = jnp.maximum(running_max, jnp.max(scores, axis=2))
    rescale = jnp.exp(running_max - new_max)
    weight_tensors = jnp.exp(scores - new_max[:, :, None])
    denominator = denominator * rescale + jnp.sum(weight_tensors, axis=2)
    accumulated = accumulated * rescale[:, :, None] + jnp.einsum(
        "ytz,zyb->ytb",
        weight_tensors,
        value_rows.astype(jnp.float32),
        precision=lax.Precision.HIGHEST,
    )
    return (new_max, denominator, accumulated)


def shards(
    tokens,
    attn_gain,
    mlp_gain,
    w_query,
    w_key,
    w_value,
    w_out,
    sink_logits,
    router,
    expert_gate,
    expert_up,
    expert_down,
    layout_map,
    real_lengths,
    routes,
):
    token_count, model_width = tokens.shape
    seq_count = lax.axis_size("seq")
    tp_count = lax.axis_size("tp")
    expert_count = router.shape[1]
    route_count = routes.shape[1]
    head_count = sink_logits.shape[0]
    proj_width = head_count * HEAD
    col_share = model_width // tp_count
    total_slots = token_count * seq_count
    prompt_count = real_lengths.shape[0]
    slot_len = total_slots // prompt_count
    stagger = token_count // 2
    capacity = max(2, min(token_count, 9 * token_count * route_count // (8 * expert_count)))
    seq_place = lax.axis_index("seq")
    tp_place = lax.axis_index("tp")
    offsets = jnp.arange(token_count, dtype=jnp.int32)
    token_index = seq_place * token_count + offsets
    prompt, position = prompt_split(token_index, slot_len, stagger, prompt_count)
    valid_token = position < length_of(prompt, real_lengths)
    normed = rms_scale(tokens.astype(jnp.float32), attn_gain).astype(jnp.bfloat16)
    stack_local = jnp.concatenate([w_query, w_key, w_value], axis=1).astype(jnp.bfloat16)
    router_local = router.astype(jnp.bfloat16)
    stack_piece = lax.all_gather(stack_local, "seq", axis=0, tiled=True)
    router_piece = lax.all_gather(router_local, "seq", axis=0, tiled=True)
    product = jnp.dot(normed, stack_piece, preferred_element_type=jnp.float32)
    router_full = router_piece
    product, router_full = (product, router_full)
    rotary_positions = position.astype(jnp.float32)
    query_rows = rotate(
        product[:, :proj_width].reshape(token_count, head_count, HEAD), rotary_positions
    ).astype(jnp.bfloat16)
    key_rows = rotate(
        product[:, proj_width : 2 * proj_width].reshape(token_count, head_count, HEAD),
        rotary_positions,
    ).astype(jnp.bfloat16)
    value_rows = (
        product[:, 2 * proj_width :].astype(jnp.bfloat16).reshape(token_count, head_count, HEAD)
    )
    softmax_state = (
        jnp.broadcast_to(sink_logits[:, None], (head_count, token_count)),
        jnp.ones((head_count, token_count), jnp.float32),
        jnp.zeros((head_count, token_count, HEAD), jnp.float32),
    )
    softmax_state = attend(
        softmax_state,
        query_rows,
        key_rows,
        value_rows,
        key_rules(token_index, token_index, slot_len, stagger, total_slots, real_lengths),
    )
    own_pair = jnp.stack([key_rows, value_rows])

    def one_turn(turn_index, loop_carry):
        loop_state, from_below, from_above = loop_carry
        from_below = from_behind(from_below, "seq", 1)
        from_above = from_behind(from_above, "seq", -1)
        reach_rows = (turn_index + 1) * token_count
        key_ids = jnp.concatenate([token_index - reach_rows, token_index + reach_rows])
        neighbours = jnp.concatenate([from_below, from_above], axis=1)
        allowed = key_rules(token_index, key_ids, slot_len, stagger, total_slots, real_lengths)
        loop_state = attend(loop_state, query_rows, neighbours[0], neighbours[1], allowed)
        return (loop_state, from_below, from_above)

    softmax_state, from_below, from_above = lax.fori_loop(
        0, HALF_WIN // token_count, one_turn, (softmax_state, own_pair, own_pair)
    )
    running_max, denominator, accumulated = softmax_state
    attention_result = (
        jnp.transpose(accumulated / denominator[:, :, None], (1, 0, 2))
        .reshape(token_count, proj_width)
        .astype(jnp.bfloat16)
    )
    partial_out = jnp.dot(
        attention_result,
        lax.all_gather(w_out.astype(jnp.bfloat16), "seq", axis=1, tiled=True),
        preferred_element_type=jnp.float32,
    )
    mixed_full = lax.psum(partial_out, "tp")
    full_rows = tokens.astype(jnp.float32) + mixed_full
    outgoing = rms_scale(full_rows, mlp_gain).astype(jnp.bfloat16)
    logits = jnp.dot(outgoing, router_full, preferred_element_type=jnp.float32)
    residual = lax.dynamic_slice_in_dim(full_rows, tp_place * col_share, col_share, 1)
    expert_ids = jnp.arange(expert_count, dtype=jnp.int32)
    chosen = routes[:, :, None] == expert_ids[None, None, :]
    route_logits = jnp.sum(jnp.where(chosen, logits[:, None, :], 0.0), axis=2)
    route_weight = jax.nn.softmax(route_logits, axis=1) * valid_token[:, None]
    flat_routes = routes.reshape(-1)
    live_route = jnp.repeat(valid_token, route_count)
    one_hot = ((flat_routes[:, None] == expert_ids[None, :]) & live_route[:, None]).astype(
        jnp.int32
    )
    rank_within = jnp.sum((jnp.cumsum(one_hot, axis=0) - one_hot) * one_hot, axis=1)
    slot_index = flat_routes * capacity + rank_within
    target_slot = jnp.where(live_route, slot_index, expert_count * capacity)
    owner_row = jnp.repeat(offsets, route_count) + 1
    source_row = (
        jnp.zeros((expert_count * capacity,), jnp.int32).at[target_slot].set(owner_row, mode="drop")
    )
    buffer = jnp.where(
        (source_row > 0)[:, None],
        outgoing[jnp.maximum(source_row - 1, 0)],
        jnp.zeros((), jnp.bfloat16),
    )
    buffer = buffer.reshape(expert_count, capacity, outgoing.shape[1])
    trainer = jnp.concatenate([expert_gate, expert_up, expert_down], axis=2).astype(jnp.bfloat16)
    ordered = jnp.take(trainer, layout_map, axis=0)
    server = lax.all_to_all(ordered, "seq", split_axis=0, concat_axis=1, tiled=True)
    hidden_share = expert_gate.shape[2]
    local_experts = server.shape[0]
    full_block = lax.all_to_all(buffer, "seq", split_axis=0, concat_axis=0, tiled=True)
    item_count = full_block.shape[1]
    grouped = full_block.reshape(seq_count, local_experts, item_count, model_width)
    gate_up = jnp.einsum(
        "sacd,adf->sacf",
        grouped,
        server[:, :, : 2 * hidden_share],
        preferred_element_type=jnp.float32,
    )
    hidden_state = (jax.nn.silu(gate_up[..., :hidden_share]) * gate_up[..., hidden_share:]).astype(
        jnp.bfloat16
    )
    partial_rows = jnp.einsum(
        "sacf,adf->sacd",
        hidden_state,
        server[:, :, 2 * hidden_share :],
        preferred_element_type=jnp.float32,
    )
    partial_rows = lax.optimization_barrier(partial_rows.astype(jnp.bfloat16)).astype(jnp.float32)
    summed = lax.psum_scatter(
        partial_rows.astype(jnp.bfloat16), "tp", scatter_dimension=3, tiled=True
    )
    returned = lax.all_to_all(
        summed.reshape(seq_count * local_experts, item_count, col_share),
        "seq",
        split_axis=0,
        concat_axis=0,
        tiled=True,
    )
    picked = returned.reshape(expert_count * capacity, col_share)[
        jnp.where(live_route, slot_index, 0)
    ]
    picked = picked.reshape(token_count, route_count, col_share)
    expert_mix = jnp.sum(route_weight[:, :, None] * picked.astype(jnp.float32), axis=1)
    return (residual + expert_mix).astype(jnp.bfloat16)


def solution(mesh):
    placed = (
        P("seq", None),
        P(),
        P(),
        P("seq", "tp"),
        P("seq", "tp"),
        P("seq", "tp"),
        P("tp", "seq"),
        P("tp"),
        P("seq", None),
        P(None, "seq", "tp"),
        P(None, "seq", "tp"),
        P(None, "seq", "tp"),
        P(),
        P(),
        P("seq", None),
    )
    return jax.shard_map(
        shards, mesh=mesh, in_specs=placed, out_specs=P("seq", "tp"), check_vma=False
    )
```

profile of v0, /device:TPU:18, one launch (start us, length us, event | category | flops | bytes accessed | tf_op | source)
XLA Modules:
  0.0 1064.2 jit_solution(7470347210897196199)
XLA Ops:
  35.2 7.2 all-to-all-start
  50.4 233.6 %all-gather.3.cloned.1.call-done = bf16[2048,3072]{1,0:T(8,128)(2,1)} async-done(((bf16[128,3072]{1,0:T(8,128)(2,1)}), bf16[2048,3072]{1,0:T(8,128)(2,1)}) %all-gather.3.cloned.1.call-update) | async-done | bytes 12582928 | tf_op jit(solution)/shard_map/all_gather | solution.py:121
  293.4 493.8 %while.25 = (s32[]{:T(128)}, f32[8,128]{1,0:T(8,128)S(1)}, f32[8,128]{1,0:T(8,128)S(1)}, f32[8,128,128]{2,1,0:T(8,128)S(1)}, bf16[2,128,8,128]{3,1,2,0:T(8,128)(...) while((s32[]{:T(128)}, f32[8,128]{1,0:T(8,128)S(1)}, ...), condition=%wide.region_8.9_spmd.clone, body=%wide.region_4.8_spmd.clone.sunk | while | flops 471806848 | bytes 14038749 | solution.py:162
  300.5 23.3 %collective-permute-done = bf16[2,128,8,128]{3,1,2,0:T(8,128)(2,1)S(1)} collective-permute-done((bf16[2,128,8,128]{3,1,2,0:T(8,128)(2,1)S(1)}, bf16[2,128,8,128]{3,1,2,0:T(8,128)(2,1)S(1)}, u32[]{:S(2)}, u32[]{:S(2)}) %collective-permute-start) | collective-permute-done | bytes 524320 | tf_op jit(solution)/shard_map/while/body/eval_jaxpr/ppermute | solution.py:16
  332.8 20.7 %collective-permute-done = bf16[2,128,8,128]{3,1,2,0:T(8,128)(2,1)S(1)} collective-permute-done((bf16[2,128,8,128]{3,1,2,0:T(8,128)(2,1)S(1)}, bf16[2,128,8,128]{3,1,2,0:T(8,128)(2,1)S(1)}, u32[]{:S(2)}, u32[]{:S(2)}) %collective-permute-start) | collective-permute-done | bytes 524320 | tf_op jit(solution)/shard_map/while/body/eval_jaxpr/ppermute | solution.py:16
  362.5 41.4 %collective-permute-done = bf16[2,128,8,128]{3,1,2,0:T(8,128)(2,1)S(1)} collective-permute-done((bf16[2,128,8,128]{3,1,2,0:T(8,128)(2,1)S(1)}, bf16[2,128,8,128]{3,1,2,0:T(8,128)(2,1)S(1)}, u32[]{:S(2)}, u32[]{:S(2)}) %collective-permute-start) | collective-permute-done | bytes 524320 | tf_op jit(solution)/shard_map/while/body/eval_jaxpr/ppermute | solution.py:16
  413.3 21.1 %collective-permute-done = bf16[2,128,8,128]{3,1,2,0:T(8,128)(2,1)S(1)} collective-permute-done((bf16[2,128,8,128]{3,1,2,0:T(8,128)(2,1)S(1)}, bf16[2,128,8,128]{3,1,2,0:T(8,128)(2,1)S(1)}, u32[]{:S(2)}, u32[]{:S(2)}) %collective-permute-start) | collective-permute-done | bytes 524320 | tf_op jit(solution)/shard_map/while/body/eval_jaxpr/ppermute | solution.py:16
  443.4 19.8 %collective-permute-done = bf16[2,128,8,128]{3,1,2,0:T(8,128)(2,1)S(1)} collective-permute-done((bf16[2,128,8,128]{3,1,2,0:T(8,128)(2,1)S(1)}, bf16[2,128,8,128]{3,1,2,0:T(8,128)(2,1)S(1)}, u32[]{:S(2)}, u32[]{:S(2)}) %collective-permute-start) | collective-permute-done | bytes 524320 | tf_op jit(solution)/shard_map/while/body/eval_jaxpr/ppermute | solution.py:16
  472.2 19.4 %collective-permute-done = bf16[2,128,8,128]{3,1,2,0:T(8,128)(2,1)S(1)} collective-permute-done((bf16[2,128,8,128]{3,1,2,0:T(8,128)(2,1)S(1)}, bf16[2,128,8,128]{3,1,2,0:T(8,128)(2,1)S(1)}, u32[]{:S(2)}, u32[]{:S(2)}) %collective-permute-start) | collective-permute-done | bytes 524320 | tf_op jit(solution)/shard_map/while/body/eval_jaxpr/ppermute | solution.py:16
  500.7 21.3 %collective-permute-done = bf16[2,128,8,128]{3,1,2,0:T(8,128)(2,1)S(1)} collective-permute-done((bf16[2,128,8,128]{3,1,2,0:T(8,128)(2,1)S(1)}, bf16[2,128,8,128]{3,1,2,0:T(8,128)(2,1)S(1)}, u32[]{:S(2)}, u32[]{:S(2)}) %collective-permute-start) | collective-permute-done | bytes 524320 | tf_op jit(solution)/shard_map/while/body/eval_jaxpr/ppermute | solution.py:16
  531.0 19.4 %collective-permute-done = bf16[2,128,8,128]{3,1,2,0:T(8,128)(2,1)S(1)} collective-permute-done((bf16[2,128,8,128]{3,1,2,0:T(8,128)(2,1)S(1)}, bf16[2,128,8,128]{3,1,2,0:T(8,128)(2,1)S(1)}, u32[]{:S(2)}, u32[]{:S(2)}) %collective-permute-start) | collective-permute-done | bytes 524320 | tf_op jit(solution)/shard_map/while/body/eval_jaxpr/ppermute | solution.py:16
  559.4 21.3 %collective-permute-done = bf16[2,128,8,128]{3,1,2,0:T(8,128)(2,1)S(1)} collective-permute-done((bf16[2,128,8,128]{3,1,2,0:T(8,128)(2,1)S(1)}, bf16[2,128,8,128]{3,1,2,0:T(8,128)(2,1)S(1)}, u32[]{:S(2)}, u32[]{:S(2)}) %collective-permute-start) | collective-permute-done | bytes 524320 | tf_op jit(solution)/shard_map/while/body/eval_jaxpr/ppermute | solution.py:16
  589.7 19.4 %collective-permute-done = bf16[2,128,8,128]{3,1,2,0:T(8,128)(2,1)S(1)} collective-permute-done((bf16[2,128,8,128]{3,1,2,0:T(8,128)(2,1)S(1)}, bf16[2,128,8,128]{3,1,2,0:T(8,128)(2,1)S(1)}, u32[]{:S(2)}, u32[]{:S(2)}) %collective-permute-start) | collective-permute-done | bytes 524320 | tf_op jit(solution)/shard_map/while/body/eval_jaxpr/ppermute | solution.py:16
  618.1 21.3 %collective-permute-done = bf16[2,128,8,128]{3,1,2,0:T(8,128)(2,1)S(1)} collective-permute-done((bf16[2,128,8,128]{3,1,2,0:T(8,128)(2,1)S(1)}, bf16[2,128,8,128]{3,1,2,0:T(8,128)(2,1)S(1)}, u32[]{:S(2)}, u32[]{:S(2)}) %collective-permute-start) | collective-permute-done | bytes 524320 | tf_op jit(solution)/shard_map/while/body/eval_jaxpr/ppermute | solution.py:16
  648.4 19.4 %collective-permute-done = bf16[2,128,8,128]{3,1,2,0:T(8,128)(2,1)S(1)} collective-permute-done((bf16[2,128,8,128]{3,1,2,0:T(8,128)(2,1)S(1)}, bf16[2,128,8,128]{3,1,2,0:T(8,128)(2,1)S(1)}, u32[]{:S(2)}, u32[]{:S(2)}) %collective-permute-start) | collective-permute-done | bytes 524320 | tf_op jit(solution)/shard_map/while/body/eval_jaxpr/ppermute | solution.py:16
  676.9 21.3 %collective-permute-done = bf16[2,128,8,128]{3,1,2,0:T(8,128)(2,1)S(1)} collective-permute-done((bf16[2,128,8,128]{3,1,2,0:T(8,128)(2,1)S(1)}, bf16[2,128,8,128]{3,1,2,0:T(8,128)(2,1)S(1)}, u32[]{:S(2)}, u32[]{:S(2)}) %collective-permute-start) | collective-permute-done | bytes 524320 | tf_op jit(solution)/shard_map/while/body/eval_jaxpr/ppermute | solution.py:16
  707.2 19.4 %collective-permute-done = bf16[2,128,8,128]{3,1,2,0:T(8,128)(2,1)S(1)} collective-permute-done((bf16[2,128,8,128]{3,1,2,0:T(8,128)(2,1)S(1)}, bf16[2,128,8,128]{3,1,2,0:T(8,128)(2,1)S(1)}, u32[]{:S(2)}, u32[]{:S(2)}) %collective-permute-start) | collective-permute-done | bytes 524320 | tf_op jit(solution)/shard_map/while/body/eval_jaxpr/ppermute | solution.py:16
  735.6 21.3 %collective-permute-done = bf16[2,128,8,128]{3,1,2,0:T(8,128)(2,1)S(1)} collective-permute-done((bf16[2,128,8,128]{3,1,2,0:T(8,128)(2,1)S(1)}, bf16[2,128,8,128]{3,1,2,0:T(8,128)(2,1)S(1)}, u32[]{:S(2)}, u32[]{:S(2)}) %collective-permute-start) | collective-permute-done | bytes 524320 | tf_op jit(solution)/shard_map/while/body/eval_jaxpr/ppermute | solution.py:16
  765.9 19.4 %collective-permute-done = bf16[2,128,8,128]{3,1,2,0:T(8,128)(2,1)S(1)} collective-permute-done((bf16[2,128,8,128]{3,1,2,0:T(8,128)(2,1)S(1)}, bf16[2,128,8,128]{3,1,2,0:T(8,128)(2,1)S(1)}, u32[]{:S(2)}, u32[]{:S(2)}) %collective-permute-start) | collective-permute-done | bytes 524320 | tf_op jit(solution)/shard_map/while/body/eval_jaxpr/ppermute | solution.py:16
  796.2 15.8 %all-reduce.2.cloned.1.call-done = f32[128,2048]{1,0:T(8,128)} async-done(((f32[128,2048]{1,0:T(8,128)}), f32[128,2048]{1,0:T(8,128)}) %all-reduce.2.cloned.1.call-update) | async-done | bytes 1048592 | tf_op jit(solution)/shard_map/psum | solution.py:176
  825.4 110.3 %all_to_all.22 = bf16[16,72,2048]{2,1,0:T(8,128)(2,1)S(1)} all-to-all(bf16[16,72,2048]{2,1,0:T(8,128)(2,1)} %broadcast_select_fusion.1), channel_id=1, replica_groups=mesh['seq'=16,'tp'=2] {'seq'}, dimensions={0} | all-to-all | bytes 9437184 | tf_op jit(solution)/shard_map/all_to_all | solution.py:208
  935.7 7.3 fusion.14
  949.0 13.0 %reduce-scatter.2.cloned.1.call-done = bf16[16,1,72,1024]{3,2,0,1:T(8,128)(2,1)} async-done(((bf16[16,1,72,2048]{3,2,0,1:T(8,128)(2,1)}), bf16[16,1,72,1024]{3,2,0,1:T(8,128)(2,1)}) %reduce-scatter.2.cloned.1.call-update) | async-done | bytes 2359312 | tf_op jit(solution)/shard_map/reduce_scatter | solution.py:227
  968.9 78.2 %all_gather.11 = bf16[2048,16]{0,1:T(8,128)(2,1)S(1)} all-gather(bf16[128,16]{0,1:T(8,128)(2,1)S(1)} %convert_element_type.94), channel_id=1, replica_groups=mesh['seq'=16,'tp'=2] {'seq'}, dimensions={0}, use_global_device_ids=true | all-gather | bytes 69632 | tf_op jit(solution)/shard_map/all_gather | solution.py:122
  (431 shorter events, 233.7 us)
Async XLA Ops:
  6.5 277.4 %all-gather.3.cloned.1.call-start = ((), (), s32[]{:S(2)}) async-start(), calls=%async_computation.4 | async-start | bytes 13369344 | tf_op jit(solution)/shard_map/all_gather | solution.py:121
  35.2 790.3 %all-to-all-start = ((bf16[16,128,1536]{2,1,0:T(8,128)(2,1)}), bf16[16,128,1536]{2,1,0:T(8,128)(2,1)}, u32[]{:S(2)}, u32[]{:S(2)}) async-start(bf16[16,128,1536]{2,1,0:T(8,128)(2,1)} %broadcast_select_fusion), calls=%async_computation | async-start | bytes 12582912 | tf_op jit(solution)/shard_map/all_to_all | solution.py:205
  42.4 745.1 %all-gather.5.cloned.1.call-start = ((), (), s32[]{:S(2)}) async-start(), calls=%async_computation.5 | async-start | bytes 4456448 | tf_op jit(solution)/shard_map/all_gather | solution.py:173
  43.2 768.7 %all-reduce.2.cloned.1.call-start = ((), (), s32[]{:S(2)}) async-start(), calls=%async_computation.6 | async-start | bytes 2097152 | tf_op jit(solution)/shard_map/psum | solution.py:176
  293.4 30.4 %collective-permute-start.1 = (bf16[2,128,8,128]{3,1,2,0:T(8,128)(2,1)S(1)}, bf16[2,128,8,128]{3,1,2,0:T(8,128)(2,1)S(1)}, u32[]{:S(2)}, u32[]{:S(2)}) collective-permute-start(bf16[2,128,8,128]{3,1,2,0:T(8,128)(2,1)S(1)} %get-tuple-element.428), channel_id=1, source_target_pairs={{2,0},{4,2},{6,4},{8,6},{10,8},{12,10},{14,12},{16,14},{18,16},{20... | collective-permute-start | bytes 1572872 | tf_op jit(solution)/shard_map/while/body/eval_jaxpr/ppermute | solution.py:16
  296.1 27.7 %collective-permute-start = (bf16[2,128,8,128]{3,1,2,0:T(8,128)(2,1)S(1)}, bf16[2,128,8,128]{3,1,2,0:T(8,128)(2,1)S(1)}, u32[]{:S(2)}, u32[]{:S(2)}) collective-permute-start(bf16[2,128,8,128]{3,1,2,0:T(8,128)(2,1)S(1)} %get-tuple-element.427), channel_id=1, source_target_pairs={{0,2},{2,4},{4,6},{6,8},{8,10},{10,12},{12,14},{14,16},{16,18},{18... | collective-permute-start | bytes 1572872 | tf_op jit(solution)/shard_map/while/body/eval_jaxpr/ppermute | solution.py:16
  325.7 27.8 %collective-permute-start.1 = (bf16[2,128,8,128]{3,1,2,0:T(8,128)(2,1)S(1)}, bf16[2,128,8,128]{3,1,2,0:T(8,128)(2,1)S(1)}, u32[]{:S(2)}, u32[]{:S(2)}) collective-permute-start(bf16[2,128,8,128]{3,1,2,0:T(8,128)(2,1)S(1)} %get-tuple-element.428), channel_id=1, source_target_pairs={{2,0},{4,2},{6,4},{8,6},{10,8},{12,10},{14,12},{16,14},{18,16},{20... | collective-permute-start | bytes 1572872 | tf_op jit(solution)/shard_map/while/body/eval_jaxpr/ppermute | solution.py:16
  355.4 48.5 %collective-permute-start.1 = (bf16[2,128,8,128]{3,1,2,0:T(8,128)(2,1)S(1)}, bf16[2,128,8,128]{3,1,2,0:T(8,128)(2,1)S(1)}, u32[]{:S(2)}, u32[]{:S(2)}) collective-permute-start(bf16[2,128,8,128]{3,1,2,0:T(8,128)(2,1)S(1)} %get-tuple-element.428), channel_id=1, source_target_pairs={{2,0},{4,2},{6,4},{8,6},{10,8},{12,10},{14,12},{16,14},{18,16},{20... | collective-permute-start | bytes 1572872 | tf_op jit(solution)/shard_map/while/body/eval_jaxpr/ppermute | solution.py:16
  359.3 44.6 %collective-permute-start = (bf16[2,128,8,128]{3,1,2,0:T(8,128)(2,1)S(1)}, bf16[2,128,8,128]{3,1,2,0:T(8,128)(2,1)S(1)}, u32[]{:S(2)}, u32[]{:S(2)}) collective-permute-start(bf16[2,128,8,128]{3,1,2,0:T(8,128)(2,1)S(1)} %get-tuple-element.427), channel_id=1, source_target_pairs={{0,2},{2,4},{4,6},{6,8},{8,10},{10,12},{12,14},{14,16},{16,18},{18... | collective-permute-start | bytes 1572872 | tf_op jit(solution)/shard_map/while/body/eval_jaxpr/ppermute | solution.py:16
  405.8 28.7 %collective-permute-start.1 = (bf16[2,128,8,128]{3,1,2,0:T(8,128)(2,1)S(1)}, bf16[2,128,8,128]{3,1,2,0:T(8,128)(2,1)S(1)}, u32[]{:S(2)}, u32[]{:S(2)}) collective-permute-start(bf16[2,128,8,128]{3,1,2,0:T(8,128)(2,1)S(1)} %get-tuple-element.428), channel_id=1, source_target_pairs={{2,0},{4,2},{6,4},{8,6},{10,8},{12,10},{14,12},{16,14},{18,16},{20... | collective-permute-start | bytes 1572872 | tf_op jit(solution)/shard_map/while/body/eval_jaxpr/ppermute | solution.py:16
  407.7 26.7 %collective-permute-start = (bf16[2,128,8,128]{3,1,2,0:T(8,128)(2,1)S(1)}, bf16[2,128,8,128]{3,1,2,0:T(8,128)(2,1)S(1)}, u32[]{:S(2)}, u32[]{:S(2)}) collective-permute-start(bf16[2,128,8,128]{3,1,2,0:T(8,128)(2,1)S(1)} %get-tuple-element.427), channel_id=1, source_target_pairs={{0,2},{2,4},{4,6},{6,8},{8,10},{10,12},{12,14},{14,16},{16,18},{18... | collective-permute-start | bytes 1572872 | tf_op jit(solution)/shard_map/while/body/eval_jaxpr/ppermute | solution.py:16
  436.3 27.0 %collective-permute-start.1 = (bf16[2,128,8,128]{3,1,2,0:T(8,128)(2,1)S(1)}, bf16[2,128,8,128]{3,1,2,0:T(8,128)(2,1)S(1)}, u32[]{:S(2)}, u32[]{:S(2)}) collective-permute-start(bf16[2,128,8,128]{3,1,2,0:T(8,128)(2,1)S(1)} %get-tuple-element.428), channel_id=1, source_target_pairs={{2,0},{4,2},{6,4},{8,6},{10,8},{12,10},{14,12},{16,14},{18,16},{20... | collective-permute-start | bytes 1572872 | tf_op jit(solution)/shard_map/while/body/eval_jaxpr/ppermute | solution.py:16
  493.6 28.4 %collective-permute-start.1 = (bf16[2,128,8,128]{3,1,2,0:T(8,128)(2,1)S(1)}, bf16[2,128,8,128]{3,1,2,0:T(8,128)(2,1)S(1)}, u32[]{:S(2)}, u32[]{:S(2)}) collective-permute-start(bf16[2,128,8,128]{3,1,2,0:T(8,128)(2,1)S(1)} %get-tuple-element.428), channel_id=1, source_target_pairs={{2,0},{4,2},{6,4},{8,6},{10,8},{12,10},{14,12},{16,14},{18,16},{20... | collective-permute-start | bytes 1572872 | tf_op jit(solution)/shard_map/while/body/eval_jaxpr/ppermute | solution.py:16
  523.9 26.6 %collective-permute-start.1 = (bf16[2,128,8,128]{3,1,2,0:T(8,128)(2,1)S(1)}, bf16[2,128,8,128]{3,1,2,0:T(8,128)(2,1)S(1)}, u32[]{:S(2)}, u32[]{:S(2)}) collective-permute-start(bf16[2,128,8,128]{3,1,2,0:T(8,128)(2,1)S(1)} %get-tuple-element.428), channel_id=1, source_target_pairs={{2,0},{4,2},{6,4},{8,6},{10,8},{12,10},{14,12},{16,14},{18,16},{20... | collective-permute-start | bytes 1572872 | tf_op jit(solution)/shard_map/while/body/eval_jaxpr/ppermute | solution.py:16
  552.3 28.4 %collective-permute-start.1 = (bf16[2,128,8,128]{3,1,2,0:T(8,128)(2,1)S(1)}, bf16[2,128,8,128]{3,1,2,0:T(8,128)(2,1)S(1)}, u32[]{:S(2)}, u32[]{:S(2)}) collective-permute-start(bf16[2,128,8,128]{3,1,2,0:T(8,128)(2,1)S(1)} %get-tuple-element.428), channel_id=1, source_target_pairs={{2,0},{4,2},{6,4},{8,6},{10,8},{12,10},{14,12},{16,14},{18,16},{20... | collective-permute-start | bytes 1572872 | tf_op jit(solution)/shard_map/while/body/eval_jaxpr/ppermute | solution.py:16
  582.6 26.6 %collective-permute-start.1 = (bf16[2,128,8,128]{3,1,2,0:T(8,128)(2,1)S(1)}, bf16[2,128,8,128]{3,1,2,0:T(8,128)(2,1)S(1)}, u32[]{:S(2)}, u32[]{:S(2)}) collective-permute-start(bf16[2,128,8,128]{3,1,2,0:T(8,128)(2,1)S(1)} %get-tuple-element.428), channel_id=1, source_target_pairs={{2,0},{4,2},{6,4},{8,6},{10,8},{12,10},{14,12},{16,14},{18,16},{20... | collective-permute-start | bytes 1572872 | tf_op jit(solution)/shard_map/while/body/eval_jaxpr/ppermute | solution.py:16
  611.0 28.4 %collective-permute-start.1 = (bf16[2,128,8,128]{3,1,2,0:T(8,128)(2,1)S(1)}, bf16[2,128,8,128]{3,1,2,0:T(8,128)(2,1)S(1)}, u32[]{:S(2)}, u32[]{:S(2)}) collective-permute-start(bf16[2,128,8,128]{3,1,2,0:T(8,128)(2,1)S(1)} %get-tuple-element.428), channel_id=1, source_target_pairs={{2,0},{4,2},{6,4},{8,6},{10,8},{12,10},{14,12},{16,14},{18,16},{20... | collective-permute-start | bytes 1572872 | tf_op jit(solution)/shard_map/while/body/eval_jaxpr/ppermute | solution.py:16
  641.3 26.6 %collective-permute-start.1 = (bf16[2,128,8,128]{3,1,2,0:T(8,128)(2,1)S(1)}, bf16[2,128,8,128]{3,1,2,0:T(8,128)(2,1)S(1)}, u32[]{:S(2)}, u32[]{:S(2)}) collective-permute-start(bf16[2,128,8,128]{3,1,2,0:T(8,128)(2,1)S(1)} %get-tuple-element.428), channel_id=1, source_target_pairs={{2,0},{4,2},{6,4},{8,6},{10,8},{12,10},{14,12},{16,14},{18,16},{20... | collective-permute-start | bytes 1572872 | tf_op jit(solution)/shard_map/while/body/eval_jaxpr/ppermute | solution.py:16
  669.8 28.4 %collective-permute-start.1 = (bf16[2,128,8,128]{3,1,2,0:T(8,128)(2,1)S(1)}, bf16[2,128,8,128]{3,1,2,0:T(8,128)(2,1)S(1)}, u32[]{:S(2)}, u32[]{:S(2)}) collective-permute-start(bf16[2,128,8,128]{3,1,2,0:T(8,128)(2,1)S(1)} %get-tuple-element.428), channel_id=1, source_target_pairs={{2,0},{4,2},{6,4},{8,6},{10,8},{12,10},{14,12},{16,14},{18,16},{20... | collective-permute-start | bytes 1572872 | tf_op jit(solution)/shard_map/while/body/eval_jaxpr/ppermute | solution.py:16
  700.1 26.6 %collective-permute-start.1 = (bf16[2,128,8,128]{3,1,2,0:T(8,128)(2,1)S(1)}, bf16[2,128,8,128]{3,1,2,0:T(8,128)(2,1)S(1)}, u32[]{:S(2)}, u32[]{:S(2)}) collective-permute-start(bf16[2,128,8,128]{3,1,2,0:T(8,128)(2,1)S(1)} %get-tuple-element.428), channel_id=1, source_target_pairs={{2,0},{4,2},{6,4},{8,6},{10,8},{12,10},{14,12},{16,14},{18,16},{20... | collective-permute-start | bytes 1572872 | tf_op jit(solution)/shard_map/while/body/eval_jaxpr/ppermute | solution.py:16
  728.5 28.4 %collective-permute-start.1 = (bf16[2,128,8,128]{3,1,2,0:T(8,128)(2,1)S(1)}, bf16[2,128,8,128]{3,1,2,0:T(8,128)(2,1)S(1)}, u32[]{:S(2)}, u32[]{:S(2)}) collective-permute-start(bf16[2,128,8,128]{3,1,2,0:T(8,128)(2,1)S(1)} %get-tuple-element.428), channel_id=1, source_target_pairs={{2,0},{4,2},{6,4},{8,6},{10,8},{12,10},{14,12},{16,14},{18,16},{20... | collective-permute-start | bytes 1572872 | tf_op jit(solution)/shard_map/while/body/eval_jaxpr/ppermute | solution.py:16
  758.8 26.6 %collective-permute-start.1 = (bf16[2,128,8,128]{3,1,2,0:T(8,128)(2,1)S(1)}, bf16[2,128,8,128]{3,1,2,0:T(8,128)(2,1)S(1)}, u32[]{:S(2)}, u32[]{:S(2)}) collective-permute-start(bf16[2,128,8,128]{3,1,2,0:T(8,128)(2,1)S(1)} %get-tuple-element.428), channel_id=1, source_target_pairs={{2,0},{4,2},{6,4},{8,6},{10,8},{12,10},{14,12},{16,14},{18,16},{20... | collective-permute-start | bytes 1572872 | tf_op jit(solution)/shard_map/while/body/eval_jaxpr/ppermute | solution.py:16
  791.5 170.5 %reduce-scatter.2.cloned.1.call-start = ((), (), s32[]{:S(2)}) async-start(), calls=%async_computation.7 | async-start | bytes 7077888 | tf_op jit(solution)/shard_map/reduce_scatter | solution.py:227
  962.0 85.6 %all-to-all-start.2 = ((bf16[16,72,1024]{2,1,0:T(8,128)(2,1)}), bf16[16,72,1024]{2,1,0:T(8,128)(2,1)S(1)}, u32[]{:S(2)}, u32[]{:S(2)}) async-start(bf16[16,72,1024]{2,1,0:T(8,128)(2,1)} %bitcast.102), calls=%async_computation.3 | async-start | bytes 4718592 | tf_op jit(solution)/shard_map/all_to_all | solution.py:230
  (26 other events, 695.1 us)
Sparse Core Ops, SparseCore 0:
  10.9 272.9 all-gather.2
  286.6 137.9 all-gather.4
  791.6 20.3 all-reduce.1
  949.1 12.8 reduce-scatter.1
where the time goes:
time: 1070 us; the launch traced here: 1060 us
  waiting for transfers between devices  612 us (57%)
  blocking collectives  188 us (18%)
  starting transfers between devices  123 us (11%)
  matrix products  48.1 us (4%)
  other arithmetic  45.3 us (4%)
  local copies, waits for them, and re-layouts  31.9 us (3%)
  between operations  13.6 us (1%)
    ppermute x32, waiting for transfers between devices, from_behind(): lax.ppermute(value, axis, [(source, source + steps) for source in range(f...  349 us
    all_gather x1, waiting for transfers between devices, shards(): stack_piece = lax.all_gather(stack_local, 'seq', axis=0, tiled=True)  234 us
    all_to_all x1, blocking collectives, shards(): lax.all_to_all(buffer, 'seq', split_axis=0, concat_axis=0, tiled=True)  110 us
    ppermute x32, starting transfers between devices, from_behind(): lax.ppermute(value, axis, [(source, source + steps) for source in range(f...  108 us
    all_gather x1, blocking collectives, shards(): router_piece = lax.all_gather(router_local, 'seq', axis=0, tiled=True)  78.2 us
  transfers between devices with their start and end apart: 38, of which 19 were waited for; matrix products, arithmetic and copies ran while one was open for 9% of the time, Pallas kernels for 0%

commit v1 on v0

--- a/solution.py
+++ b/solution.py
@@ -8,6 +8,18 @@
 EPSILON = 1e-05
 ROPE_BASE = 50000.0
 MASKED = -1e30
+
+
+def collect(value, axis, dim):
+    ways, here, lap = (lax.axis_size(axis), lax.axis_index(axis), value.shape[dim])
+    line, have = (value, 1)
+    while have < ways:
+        line = jnp.concatenate(
+            [line, lax.ppermute(line, axis, [(d, (d - have) % ways) for d in range(ways)])],
+            axis=dim,
+        )
+        have = 2 * have
+    return jnp.roll(line, here * lap, axis=dim)
 
 
 def from_behind(value, axis, steps):
@@ -119,7 +131,7 @@
     stack_local = jnp.concatenate([w_query, w_key, w_value], axis=1).astype(jnp.bfloat16)
     router_local = router.astype(jnp.bfloat16)
     stack_piece = lax.all_gather(stack_local, "seq", axis=0, tiled=True)
-    router_piece = lax.all_gather(router_local, "seq", axis=0, tiled=True)
+    router_piece = collect(router_local, "seq", 0)
     product = jnp.dot(normed, stack_piece, preferred_element_type=jnp.float32)
     router_full = router_piece
     product, router_full = (product, router_full)

time: 1070 us -> 1050 us (0.981)
  blocking collectives: 188 us -> 110 us
  starting transfers between devices: 123 us -> 168 us
  waiting for transfers between devices: 612 us -> 631 us
    all_gather x1 -> x0, blocking collectives: 78.2 us -> none  [shards(): router_piece = lax.all_gather(router_local, 'seq', axis=0, tiled=True)]
    ppermute x0 -> x4, starting transfers between devices: none -> 45.2 us  [collect(): lax.ppermute(line, axis, [(d, (d - have) % ways) for d in range(ways)])]
    ppermute x0 -> x4, waiting for transfers between devices: none -> 19.3 us  [collect(): lax.ppermute(line, axis, [(d, (d - have) % ways) for d in range(ways)])]
  transfers between devices with their start and end apart: 38 -> 42, of which waited for: 19 -> 23; matrix products, arithmetic and copies ran while one was open for 9% -> 9% of each run, Pallas kernels for 0% -> 0%
where the time goes in v1:
time: 1050 us
  waiting for transfers between devices  631 us (60%)
  starting transfers between devices  168 us (16%)
  blocking collectives  110 us (10%)
  matrix products  48.1 us (5%)
  other arithmetic  45.3 us (4%)
  local copies, waits for them, and re-layouts  32 us (3%)
  between operations  13.6 us (1%)
    ppermute x32, waiting for transfers between devices, from_behind(): lax.ppermute(value, axis, [(source, source + steps) for source in range(f...  350 us
    all_gather x1, waiting for transfers between devices, shards(): stack_piece = lax.all_gather(stack_local, 'seq', axis=0, tiled=True)  234 us
    all_to_all x1, blocking collectives, shards(): lax.all_to_all(buffer, 'seq', split_axis=0, concat_axis=0, tiled=True)  110 us
    ppermute x32, starting transfers between devices, from_behind(): lax.ppermute(value, axis, [(source, source + steps) for source in range(f...  108 us
    ppermute x4, starting transfers between devices, collect(): lax.ppermute(line, axis, [(d, (d - have) % ways) for d in range(ways)])  45.2 us
  transfers between devices with their start and end apart: 42, of which 23 were waited for; matrix products, arithmetic and copies ran while one was open for 9% of the time, Pallas kernels for 0%

profile of v1, /device:TPU:18, one launch (start us, length us, event | category | flops | bytes accessed | tf_op | source)
XLA Modules:
  0.0 1050.6 jit_solution(6517056091628822973)
XLA Ops:
  50.4 233.6 %all-gather.3.cloned.1.call-done = bf16[2048,3072]{1,0:T(8,128)(2,1)} async-done(((bf16[128,3072]{1,0:T(8,128)(2,1)}), bf16[2048,3072]{1,0:T(8,128)(2,1)}) %all-gather.3.cloned.1.call-update) | async-done | bytes 12582928 | tf_op jit(solution)/shard_map/all_gather | solution.py:133
  293.4 493.9 %while.25 = (s32[]{:T(128)}, f32[8,128]{1,0:T(8,128)S(1)}, f32[8,128]{1,0:T(8,128)S(1)}, f32[8,128,128]{2,1,0:T(8,128)S(1)}, bf16[2,128,8,128]{3,1,2,0:T(8,128)(...) while((s32[]{:T(128)}, f32[8,128]{1,0:T(8,128)S(1)}, ...), condition=%wide.region_8.9_spmd.clone, body=%wide.region_4.8_spmd.clone.sunk | while | flops 471806848 | bytes 14038749 | solution.py:174
  300.5 23.3 %collective-permute-done = bf16[2,128,8,128]{3,1,2,0:T(8,128)(2,1)S(1)} collective-permute-done((bf16[2,128,8,128]{3,1,2,0:T(8,128)(2,1)S(1)}, bf16[2,128,8,128]{3,1,2,0:T(8,128)(2,1)S(1)}, u32[]{:S(2)}, u32[]{:S(2)}) %collective-permute-start) | collective-permute-done | bytes 524320 | tf_op jit(solution)/shard_map/while/body/eval_jaxpr/ppermute | solution.py:28
  332.8 20.7 %collective-permute-done = bf16[2,128,8,128]{3,1,2,0:T(8,128)(2,1)S(1)} collective-permute-done((bf16[2,128,8,128]{3,1,2,0:T(8,128)(2,1)S(1)}, bf16[2,128,8,128]{3,1,2,0:T(8,128)(2,1)S(1)}, u32[]{:S(2)}, u32[]{:S(2)}) %collective-permute-start) | collective-permute-done | bytes 524320 | tf_op jit(solution)/shard_map/while/body/eval_jaxpr/ppermute | solution.py:28
  362.5 41.4 %collective-permute-done = bf16[2,128,8,128]{3,1,2,0:T(8,128)(2,1)S(1)} collective-permute-done((bf16[2,128,8,128]{3,1,2,0:T(8,128)(2,1)S(1)}, bf16[2,128,8,128]{3,1,2,0:T(8,128)(2,1)S(1)}, u32[]{:S(2)}, u32[]{:S(2)}) %collective-permute-start) | collective-permute-done | bytes 524320 | tf_op jit(solution)/shard_map/while/body/eval_jaxpr/ppermute | solution.py:28
  413.3 21.1 %collective-permute-done = bf16[2,128,8,128]{3,1,2,0:T(8,128)(2,1)S(1)} collective-permute-done((bf16[2,128,8,128]{3,1,2,0:T(8,128)(2,1)S(1)}, bf16[2,128,8,128]{3,1,2,0:T(8,128)(2,1)S(1)}, u32[]{:S(2)}, u32[]{:S(2)}) %collective-permute-start) | collective-permute-done | bytes 524320 | tf_op jit(solution)/shard_map/while/body/eval_jaxpr/ppermute | solution.py:28
  443.5 19.8 %collective-permute-done = bf16[2,128,8,128]{3,1,2,0:T(8,128)(2,1)S(1)} collective-permute-done((bf16[2,128,8,128]{3,1,2,0:T(8,128)(2,1)S(1)}, bf16[2,128,8,128]{3,1,2,0:T(8,128)(2,1)S(1)}, u32[]{:S(2)}, u32[]{:S(2)}) %collective-permute-start) | collective-permute-done | bytes 524320 | tf_op jit(solution)/shard_map/while/body/eval_jaxpr/ppermute | solution.py:28
  472.2 19.5 %collective-permute-done = bf16[2,128,8,128]{3,1,2,0:T(8,128)(2,1)S(1)} collective-permute-done((bf16[2,128,8,128]{3,1,2,0:T(8,128)(2,1)S(1)}, bf16[2,128,8,128]{3,1,2,0:T(8,128)(2,1)S(1)}, u32[]{:S(2)}, u32[]{:S(2)}) %collective-permute-start) | collective-permute-done | bytes 524320 | tf_op jit(solution)/shard_map/while/body/eval_jaxpr/ppermute | solution.py:28
  500.7 21.2 %collective-permute-done = bf16[2,128,8,128]{3,1,2,0:T(8,128)(2,1)S(1)} collective-permute-done((bf16[2,128,8,128]{3,1,2,0:T(8,128)(2,1)S(1)}, bf16[2,128,8,128]{3,1,2,0:T(8,128)(2,1)S(1)}, u32[]{:S(2)}, u32[]{:S(2)}) %collective-permute-start) | collective-permute-done | bytes 524320 | tf_op jit(solution)/shard_map/while/body/eval_jaxpr/ppermute | solution.py:28
  530.9 19.5 %collective-permute-done = bf16[2,128,8,128]{3,1,2,0:T(8,128)(2,1)S(1)} collective-permute-done((bf16[2,128,8,128]{3,1,2,0:T(8,128)(2,1)S(1)}, bf16[2,128,8,128]{3,1,2,0:T(8,128)(2,1)S(1)}, u32[]{:S(2)}, u32[]{:S(2)}) %collective-permute-start) | collective-permute-done | bytes 524320 | tf_op jit(solution)/shard_map/while/body/eval_jaxpr/ppermute | solution.py:28
  559.5 21.2 %collective-permute-done = bf16[2,128,8,128]{3,1,2,0:T(8,128)(2,1)S(1)} collective-permute-done((bf16[2,128,8,128]{3,1,2,0:T(8,128)(2,1)S(1)}, bf16[2,128,8,128]{3,1,2,0:T(8,128)(2,1)S(1)}, u32[]{:S(2)}, u32[]{:S(2)}) %collective-permute-start) | collective-permute-done | bytes 524320 | tf_op jit(solution)/shard_map/while/body/eval_jaxpr/ppermute | solution.py:28
  589.7 19.5 %collective-permute-done = bf16[2,128,8,128]{3,1,2,0:T(8,128)(2,1)S(1)} collective-permute-done((bf16[2,128,8,128]{3,1,2,0:T(8,128)(2,1)S(1)}, bf16[2,128,8,128]{3,1,2,0:T(8,128)(2,1)S(1)}, u32[]{:S(2)}, u32[]{:S(2)}) %collective-permute-start) | collective-permute-done | bytes 524320 | tf_op jit(solution)/shard_map/while/body/eval_jaxpr/ppermute | solution.py:28
  618.2 21.2 %collective-permute-done = bf16[2,128,8,128]{3,1,2,0:T(8,128)(2,1)S(1)} collective-permute-done((bf16[2,128,8,128]{3,1,2,0:T(8,128)(2,1)S(1)}, bf16[2,128,8,128]{3,1,2,0:T(8,128)(2,1)S(1)}, u32[]{:S(2)}, u32[]{:S(2)}) %collective-permute-start) | collective-permute-done | bytes 524320 | tf_op jit(solution)/shard_map/while/body/eval_jaxpr/ppermute | solution.py:28
  648.4 19.5 %collective-permute-done = bf16[2,128,8,128]{3,1,2,0:T(8,128)(2,1)S(1)} collective-permute-done((bf16[2,128,8,128]{3,1,2,0:T(8,128)(2,1)S(1)}, bf16[2,128,8,128]{3,1,2,0:T(8,128)(2,1)S(1)}, u32[]{:S(2)}, u32[]{:S(2)}) %collective-permute-start) | collective-permute-done | bytes 524320 | tf_op jit(solution)/shard_map/while/body/eval_jaxpr/ppermute | solution.py:28
  676.9 21.2 %collective-permute-done = bf16[2,128,8,128]{3,1,2,0:T(8,128)(2,1)S(1)} collective-permute-done((bf16[2,128,8,128]{3,1,2,0:T(8,128)(2,1)S(1)}, bf16[2,128,8,128]{3,1,2,0:T(8,128)(2,1)S(1)}, u32[]{:S(2)}, u32[]{:S(2)}) %collective-permute-start) | collective-permute-done | bytes 524320 | tf_op jit(solution)/shard_map/while/body/eval_jaxpr/ppermute | solution.py:28
  707.1 19.5 %collective-permute-done = bf16[2,128,8,128]{3,1,2,0:T(8,128)(2,1)S(1)} collective-permute-done((bf16[2,128,8,128]{3,1,2,0:T(8,128)(2,1)S(1)}, bf16[2,128,8,128]{3,1,2,0:T(8,128)(2,1)S(1)}, u32[]{:S(2)}, u32[]{:S(2)}) %collective-permute-start) | collective-permute-done | bytes 524320 | tf_op jit(solution)/shard_map/while/body/eval_jaxpr/ppermute | solution.py:28
  735.7 21.2 %collective-permute-done = bf16[2,128,8,128]{3,1,2,0:T(8,128)(2,1)S(1)} collective-permute-done((bf16[2,128,8,128]{3,1,2,0:T(8,128)(2,1)S(1)}, bf16[2,128,8,128]{3,1,2,0:T(8,128)(2,1)S(1)}, u32[]{:S(2)}, u32[]{:S(2)}) %collective-permute-start) | collective-permute-done | bytes 524320 | tf_op jit(solution)/shard_map/while/body/eval_jaxpr/ppermute | solution.py:28
  765.9 19.5 %collective-permute-done = bf16[2,128,8,128]{3,1,2,0:T(8,128)(2,1)S(1)} collective-permute-done((bf16[2,128,8,128]{3,1,2,0:T(8,128)(2,1)S(1)}, bf16[2,128,8,128]{3,1,2,0:T(8,128)(2,1)S(1)}, u32[]{:S(2)}, u32[]{:S(2)}) %collective-permute-start) | collective-permute-done | bytes 524320 | tf_op jit(solution)/shard_map/while/body/eval_jaxpr/ppermute | solution.py:28
  796.2 15.7 %all-reduce.2.cloned.1.call-done = f32[128,2048]{1,0:T(8,128)} async-done(((f32[128,2048]{1,0:T(8,128)}), f32[128,2048]{1,0:T(8,128)}) %all-reduce.2.cloned.1.call-update) | async-done | bytes 1048592 | tf_op jit(solution)/shard_map/psum | solution.py:188
  825.4 110.3 %all_to_all.22 = bf16[16,72,2048]{2,1,0:T(8,128)(2,1)S(1)} all-to-all(bf16[16,72,2048]{2,1,0:T(8,128)(2,1)} %broadcast_select_fusion.1), channel_id=1, replica_groups=mesh['seq'=16,'tp'=2] {'seq'}, dimensions={0} | all-to-all | bytes 9437184 | tf_op jit(solution)/shard_map/all_to_all | solution.py:220
  935.7 7.3 fusion.14
  949.0 13.0 %reduce-scatter.2.cloned.1.call-done = bf16[16,1,72,1024]{3,2,0,1:T(8,128)(2,1)} async-done(((bf16[16,1,72,2048]{3,2,0,1:T(8,128)(2,1)}), bf16[16,1,72,1024]{3,2,0,1:T(8,128)(2,1)}) %reduce-scatter.2.cloned.1.call-update) | async-done | bytes 2359312 | tf_op jit(solution)/shard_map/reduce_scatter | solution.py:239
  969.5 10.4 collective-permute-done.2
  979.9 43.5 %collective-permute-start.3 = (bf16[256,16]{0,1:T(8,128)(2,1)S(1)}, bf16[256,16]{0,1:T(8,128)(2,1)S(1)}, u32[]{:S(2)}, u32[]{:S(2)}) collective-permute-start(bf16[256,16]{0,1:T(8,128)(2,1)S(1)} %pad_maximum_fusion.6), channel_id=1, source_target_pairs={{0,28},{2,30},{4,0},{6,2},{8,4},{10,6},{12,8},{14,10},{16,12},{18,... | collective-permute-start | bytes 24584 | tf_op jit(solution)/shard_map/ppermute | solution.py:18
  (450 shorter events, 251.5 us)
Async XLA Ops:
  6.5 277.4 %all-gather.3.cloned.1.call-start = ((), (), s32[]{:S(2)}) async-start(), calls=%async_computation.4 | async-start | bytes 13369344 | tf_op jit(solution)/shard_map/all_gather | solution.py:133
  35.2 790.2 %all-to-all-start = ((bf16[16,128,1536]{2,1,0:T(8,128)(2,1)}), bf16[16,128,1536]{2,1,0:T(8,128)(2,1)}, u32[]{:S(2)}, u32[]{:S(2)}) async-start(bf16[16,128,1536]{2,1,0:T(8,128)(2,1)} %broadcast_select_fusion), calls=%async_computation | async-start | bytes 12582912 | tf_op jit(solution)/shard_map/all_to_all | solution.py:217
  42.4 745.2 %all-gather.5.cloned.1.call-start = ((), (), s32[]{:S(2)}) async-start(), calls=%async_computation.5 | async-start | bytes 4456448 | tf_op jit(solution)/shard_map/all_gather | solution.py:185
  43.2 768.7 %all-reduce.2.cloned.1.call-start = ((), (), s32[]{:S(2)}) async-start(), calls=%async_computation.6 | async-start | bytes 2097152 | tf_op jit(solution)/shard_map/psum | solution.py:188
  293.4 30.4 %collective-permute-start.1 = (bf16[2,128,8,128]{3,1,2,0:T(8,128)(2,1)S(1)}, bf16[2,128,8,128]{3,1,2,0:T(8,128)(2,1)S(1)}, u32[]{:S(2)}, u32[]{:S(2)}) collective-permute-start(bf16[2,128,8,128]{3,1,2,0:T(8,128)(2,1)S(1)} %get-tuple-element.430), channel_id=1, source_target_pairs={{2,0},{4,2},{6,4},{8,6},{10,8},{12,10},{14,12},{16,14},{18,16},{20... | collective-permute-start | bytes 1572872 | tf_op jit(solution)/shard_map/while/body/eval_jaxpr/ppermute | solution.py:28
  296.1 27.7 %collective-permute-start = (bf16[2,128,8,128]{3,1,2,0:T(8,128)(2,1)S(1)}, bf16[2,128,8,128]{3,1,2,0:T(8,128)(2,1)S(1)}, u32[]{:S(2)}, u32[]{:S(2)}) collective-permute-start(bf16[2,128,8,128]{3,1,2,0:T(8,128)(2,1)S(1)} %get-tuple-element.429), channel_id=1, source_target_pairs={{0,2},{2,4},{4,6},{6,8},{8,10},{10,12},{12,14},{14,16},{16,18},{18... | collective-permute-start | bytes 1572872 | tf_op jit(solution)/shard_map/while/body/eval_jaxpr/ppermute | solution.py:28
  325.7 27.8 %collective-permute-start.1 = (bf16[2,128,8,128]{3,1,2,0:T(8,128)(2,1)S(1)}, bf16[2,128,8,128]{3,1,2,0:T(8,128)(2,1)S(1)}, u32[]{:S(2)}, u32[]{:S(2)}) collective-permute-start(bf16[2,128,8,128]{3,1,2,0:T(8,128)(2,1)S(1)} %get-tuple-element.430), channel_id=1, source_target_pairs={{2,0},{4,2},{6,4},{8,6},{10,8},{12,10},{14,12},{16,14},{18,16},{20... | collective-permute-start | bytes 1572872 | tf_op jit(solution)/shard_map/while/body/eval_jaxpr/ppermute | solution.py:28
  355.4 48.5 %collective-permute-start.1 = (bf16[2,128,8,128]{3,1,2,0:T(8,128)(2,1)S(1)}, bf16[2,128,8,128]{3,1,2,0:T(8,128)(2,1)S(1)}, u32[]{:S(2)}, u32[]{:S(2)}) collective-permute-start(bf16[2,128,8,128]{3,1,2,0:T(8,128)(2,1)S(1)} %get-tuple-element.430), channel_id=1, source_target_pairs={{2,0},{4,2},{6,4},{8,6},{10,8},{12,10},{14,12},{16,14},{18,16},{20... | collective-permute-start | bytes 1572872 | tf_op jit(solution)/shard_map/while/body/eval_jaxpr/ppermute | solution.py:28
  359.2 44.6 %collective-permute-start = (bf16[2,128,8,128]{3,1,2,0:T(8,128)(2,1)S(1)}, bf16[2,128,8,128]{3,1,2,0:T(8,128)(2,1)S(1)}, u32[]{:S(2)}, u32[]{:S(2)}) collective-permute-start(bf16[2,128,8,128]{3,1,2,0:T(8,128)(2,1)S(1)} %get-tuple-element.429), channel_id=1, source_target_pairs={{0,2},{2,4},{4,6},{6,8},{8,10},{10,12},{12,14},{14,16},{16,18},{18... | collective-permute-start | bytes 1572872 | tf_op jit(solution)/shard_map/while/body/eval_jaxpr/ppermute | solution.py:28
  405.8 28.7 %collective-permute-start.1 = (bf16[2,128,8,128]{3,1,2,0:T(8,128)(2,1)S(1)}, bf16[2,128,8,128]{3,1,2,0:T(8,128)(2,1)S(1)}, u32[]{:S(2)}, u32[]{:S(2)}) collective-permute-start(bf16[2,128,8,128]{3,1,2,0:T(8,128)(2,1)S(1)} %get-tuple-element.430), channel_id=1, source_target_pairs={{2,0},{4,2},{6,4},{8,6},{10,8},{12,10},{14,12},{16,14},{18,16},{20... | collective-permute-start | bytes 1572872 | tf_op jit(solution)/shard_map/while/body/eval_jaxpr/ppermute | solution.py:28
  407.7 26.8 %collective-permute-start = (bf16[2,128,8,128]{3,1,2,0:T(8,128)(2,1)S(1)}, bf16[2,128,8,128]{3,1,2,0:T(8,128)(2,1)S(1)}, u32[]{:S(2)}, u32[]{:S(2)}) collective-permute-start(bf16[2,128,8,128]{3,1,2,0:T(8,128)(2,1)S(1)} %get-tuple-element.429), channel_id=1, source_target_pairs={{0,2},{2,4},{4,6},{6,8},{8,10},{10,12},{12,14},{14,16},{16,18},{18... | collective-permute-start | bytes 1572872 | tf_op jit(solution)/shard_map/while/body/eval_jaxpr/ppermute | solution.py:28
  436.4 26.9 %collective-permute-start.1 = (bf16[2,128,8,128]{3,1,2,0:T(8,128)(2,1)S(1)}, bf16[2,128,8,128]{3,1,2,0:T(8,128)(2,1)S(1)}, u32[]{:S(2)}, u32[]{:S(2)}) collective-permute-start(bf16[2,128,8,128]{3,1,2,0:T(8,128)(2,1)S(1)} %get-tuple-element.430), channel_id=1, source_target_pairs={{2,0},{4,2},{6,4},{8,6},{10,8},{12,10},{14,12},{16,14},{18,16},{20... | collective-permute-start | bytes 1572872 | tf_op jit(solution)/shard_map/while/body/eval_jaxpr/ppermute | solution.py:28
  493.6 28.3 %collective-permute-start.1 = (bf16[2,128,8,128]{3,1,2,0:T(8,128)(2,1)S(1)}, bf16[2,128,8,128]{3,1,2,0:T(8,128)(2,1)S(1)}, u32[]{:S(2)}, u32[]{:S(2)}) collective-permute-start(bf16[2,128,8,128]{3,1,2,0:T(8,128)(2,1)S(1)} %get-tuple-element.430), channel_id=1, source_target_pairs={{2,0},{4,2},{6,4},{8,6},{10,8},{12,10},{14,12},{16,14},{18,16},{20... | collective-permute-start | bytes 1572872 | tf_op jit(solution)/shard_map/while/body/eval_jaxpr/ppermute | solution.py:28
  552.4 28.3 %collective-permute-start.1 = (bf16[2,128,8,128]{3,1,2,0:T(8,128)(2,1)S(1)}, bf16[2,128,8,128]{3,1,2,0:T(8,128)(2,1)S(1)}, u32[]{:S(2)}, u32[]{:S(2)}) collective-permute-start(bf16[2,128,8,128]{3,1,2,0:T(8,128)(2,1)S(1)} %get-tuple-element.430), channel_id=1, source_target_pairs={{2,0},{4,2},{6,4},{8,6},{10,8},{12,10},{14,12},{16,14},{18,16},{20... | collective-permute-start | bytes 1572872 | tf_op jit(solution)/shard_map/while/body/eval_jaxpr/ppermute | solution.py:28
  582.6 26.7 %collective-permute-start.1 = (bf16[2,128,8,128]{3,1,2,0:T(8,128)(2,1)S(1)}, bf16[2,128,8,128]{3,1,2,0:T(8,128)(2,1)S(1)}, u32[]{:S(2)}, u32[]{:S(2)}) collective-permute-start(bf16[2,128,8,128]{3,1,2,0:T(8,128)(2,1)S(1)} %get-tuple-element.430), channel_id=1, source_target_pairs={{2,0},{4,2},{6,4},{8,6},{10,8},{12,10},{14,12},{16,14},{18,16},{20... | collective-permute-start | bytes 1572872 | tf_op jit(solution)/shard_map/while/body/eval_jaxpr/ppermute | solution.py:28
  611.1 28.3 %collective-permute-start.1 = (bf16[2,128,8,128]{3,1,2,0:T(8,128)(2,1)S(1)}, bf16[2,128,8,128]{3,1,2,0:T(8,128)(2,1)S(1)}, u32[]{:S(2)}, u32[]{:S(2)}) collective-permute-start(bf16[2,128,8,128]{3,1,2,0:T(8,128)(2,1)S(1)} %get-tuple-element.430), channel_id=1, source_target_pairs={{2,0},{4,2},{6,4},{8,6},{10,8},{12,10},{14,12},{16,14},{18,16},{20... | collective-permute-start | bytes 1572872 | tf_op jit(solution)/shard_map/while/body/eval_jaxpr/ppermute | solution.py:28
  641.3 26.7 %collective-permute-start.1 = (bf16[2,128,8,128]{3,1,2,0:T(8,128)(2,1)S(1)}, bf16[2,128,8,128]{3,1,2,0:T(8,128)(2,1)S(1)}, u32[]{:S(2)}, u32[]{:S(2)}) collective-permute-start(bf16[2,128,8,128]{3,1,2,0:T(8,128)(2,1)S(1)} %get-tuple-element.430), channel_id=1, source_target_pairs={{2,0},{4,2},{6,4},{8,6},{10,8},{12,10},{14,12},{16,14},{18,16},{20... | collective-permute-start | bytes 1572872 | tf_op jit(solution)/shard_map/while/body/eval_jaxpr/ppermute | solution.py:28
  669.9 28.3 %collective-permute-start.1 = (bf16[2,128,8,128]{3,1,2,0:T(8,128)(2,1)S(1)}, bf16[2,128,8,128]{3,1,2,0:T(8,128)(2,1)S(1)}, u32[]{:S(2)}, u32[]{:S(2)}) collective-permute-start(bf16[2,128,8,128]{3,1,2,0:T(8,128)(2,1)S(1)} %get-tuple-element.430), channel_id=1, source_target_pairs={{2,0},{4,2},{6,4},{8,6},{10,8},{12,10},{14,12},{16,14},{18,16},{20... | collective-permute-start | bytes 1572872 | tf_op jit(solution)/shard_map/while/body/eval_jaxpr/ppermute | solution.py:28
  700.1 26.7 %collective-permute-start.1 = (bf16[2,128,8,128]{3,1,2,0:T(8,128)(2,1)S(1)}, bf16[2,128,8,128]{3,1,2,0:T(8,128)(2,1)S(1)}, u32[]{:S(2)}, u32[]{:S(2)}) collective-permute-start(bf16[2,128,8,128]{3,1,2,0:T(8,128)(2,1)S(1)} %get-tuple-element.430), channel_id=1, source_target_pairs={{2,0},{4,2},{6,4},{8,6},{10,8},{12,10},{14,12},{16,14},{18,16},{20... | collective-permute-start | bytes 1572872 | tf_op jit(solution)/shard_map/while/body/eval_jaxpr/ppermute | solution.py:28
  728.6 28.3 %collective-permute-start.1 = (bf16[2,128,8,128]{3,1,2,0:T(8,128)(2,1)S(1)}, bf16[2,128,8,128]{3,1,2,0:T(8,128)(2,1)S(1)}, u32[]{:S(2)}, u32[]{:S(2)}) collective-permute-start(bf16[2,128,8,128]{3,1,2,0:T(8,128)(2,1)S(1)} %get-tuple-element.430), channel_id=1, source_target_pairs={{2,0},{4,2},{6,4},{8,6},{10,8},{12,10},{14,12},{16,14},{18,16},{20... | collective-permute-start | bytes 1572872 | tf_op jit(solution)/shard_map/while/body/eval_jaxpr/ppermute | solution.py:28
  758.8 26.7 %collective-permute-start.1 = (bf16[2,128,8,128]{3,1,2,0:T(8,128)(2,1)S(1)}, bf16[2,128,8,128]{3,1,2,0:T(8,128)(2,1)S(1)}, u32[]{:S(2)}, u32[]{:S(2)}) collective-permute-start(bf16[2,128,8,128]{3,1,2,0:T(8,128)(2,1)S(1)} %get-tuple-element.430), channel_id=1, source_target_pairs={{2,0},{4,2},{6,4},{8,6},{10,8},{12,10},{14,12},{16,14},{18,16},{20... | collective-permute-start | bytes 1572872 | tf_op jit(solution)/shard_map/while/body/eval_jaxpr/ppermute | solution.py:28
  791.6 170.4 %reduce-scatter.2.cloned.1.call-start = ((), (), s32[]{:S(2)}) async-start(), calls=%async_computation.7 | async-start | bytes 7077888 | tf_op jit(solution)/shard_map/reduce_scatter | solution.py:239
  961.9 72.0 %all-to-all-start.2 = ((bf16[16,72,1024]{2,1,0:T(8,128)(2,1)}), bf16[16,72,1024]{2,1,0:T(8,128)(2,1)S(1)}, u32[]{:S(2)}, u32[]{:S(2)}) async-start(bf16[16,72,1024]{2,1,0:T(8,128)(2,1)} %bitcast.101), calls=%async_computation.3 | async-start | bytes 4718592 | tf_op jit(solution)/shard_map/all_to_all | solution.py:242
  979.9 44.9 %collective-permute-start.3 = (bf16[256,16]{0,1:T(8,128)(2,1)S(1)}, bf16[256,16]{0,1:T(8,128)(2,1)S(1)}, u32[]{:S(2)}, u32[]{:S(2)}) collective-permute-start(bf16[256,16]{0,1:T(8,128)(2,1)S(1)} %pad_maximum_fusion.6), channel_id=1, source_target_pairs={{0,28},{2,30},{4,0},{6,2},{8,4},{10,6},{12,8},{14,10},{16,12},{18,... | collective-permute-start | bytes 24584 | tf_op jit(solution)/shard_map/ppermute | solution.py:18
  (30 other events, 741.4 us)
Sparse Core Ops, SparseCore 0:
  10.9 273.0 all-gather.2
  286.6 137.9 all-gather.4
  791.7 20.2 all-reduce.1
  949.1 12.8 reduce-scatter.1
